TPU v7x, 32 devices: a whole 2x2x4 slice. The times are simulated.
32 devices in a mesh: groups: 2 (over y), dap: 4 (over z), chan: 2 (over x), sub: 2 (over core).
Axes of the slice: x: 2, y: 2, z: 4, core: 2. Of those that a mesh axis runs over, the one named last changes fastest.
Arguments:
- pair_input: bfloat16 [768, 384, 128], P(('groups', 'dap'), ('chan', 'sub')), parts along dimension 0, may hold values from -6 to 6
- first_gain: float32 [128], replicated, may hold values from 0.25 to 1.75
- first_project: bfloat16 [128, 512], replicated, may hold values from -0.5 to 0.5
- first_gate: bfloat16 [128, 128], replicated, may hold values from -0.5 to 0.5
- first_norm: float32 [128], replicated, may hold values from 0.25 to 1.75
- first_final: bfloat16 [128, 128], replicated, may hold values from -0.5 to 0.5
- second_gain: float32 [128], replicated, may hold values from 0.25 to 1.75
- second_project: bfloat16 [128, 512], replicated, may hold values from -0.5 to 0.5
- second_gate: bfloat16 [128, 128], replicated, may hold values from -0.5 to 0.5
- second_norm: float32 [128], replicated, may hold values from 0.25 to 1.75
- second_final: bfloat16 [128, 128], replicated, may hold values from -0.5 to 0.5
Outputs:
- pair_output: bfloat16 [768, 384, 128], P(('groups', 'dap'), ('chan', 'sub')), parts along dimension 0
There are 2 independent parts, one for each index of `groups`. A program takes and returns all parts, laid end to end along the dimension named above; an argument that names none is the same for every part. Nothing has to cross between parts.
All inputs are finite; a program needn't handle non-finite values.
Results may differ from a plain program's by a relative error of at most 0.013.
Values may be sent and summed in bfloat16 or wider, within the bound.
No kernel may reach another device: no remote copies, remote signals or barrier semaphores. Data moves between devices by JAX's collectives and lax.ppermute only.
A program may use at most 64 MiB of HBM per device.

v0:
```python
import functools

import jax
import jax.numpy as jnp
from jax import lax
from jax.experimental import pallas as pl
from jax.experimental.pallas import tpu as pltpu
from jax.sharding import Mesh
from jax.sharding import PartitionSpec as P


epsilon = 1e-05
EVERY = ("near", "chan", "sub")
LANES = 128
BUDGET = 56 << 20


def layer_norm(values, norm_gain, reduce_axis):
    average = jnp.mean(values, axis=reduce_axis, keepdims=True)
    centred = values - average
    variance = jnp.mean(centred * centred, axis=reduce_axis, keepdims=True)
    return centred * lax.rsqrt(variance + epsilon) * norm_gain


def sigmoid(values):
    return 0.5 * jnp.tanh(0.5 * values) + 0.5


def project_in(pair_state, norm_gain, project, gate_matrix):
    features = pair_state.shape[-1]
    flattened = pair_state.reshape(-1, features).astype(jnp.float32)
    normed = layer_norm(flattened, norm_gain, 1).astype(jnp.bfloat16)
    projected = jnp.einsum("xc,cd->dx", normed, project, preferred_element_type=jnp.float32)
    left_part = jax.nn.sigmoid(projected[:features]) * projected[features : 2 * features]
    right_part = jax.nn.sigmoid(projected[2 * features : 3 * features]) * projected[3 * features :]
    gating = jax.nn.sigmoid(jnp.dot(normed, gate_matrix, preferred_element_type=jnp.float32))
    return left_part.astype(jnp.bfloat16), right_part.astype(jnp.bfloat16), gating


def finish(pair_state, mixture, gating, out_gain, final_matrix):
    features = mixture.shape[0]
    flattened = mixture.astype(jnp.float32)
    normed = layer_norm(flattened, out_gain[:, None], 0).astype(jnp.bfloat16)
    update = jnp.einsum("cx,cd->xd", normed, final_matrix, preferred_element_type=jnp.float32)
    result = pair_state.reshape(-1, features).astype(jnp.float32) + gating * update
    return result.astype(jnp.bfloat16).reshape(pair_state.shape)


def update(incoming, sizes, pair_state, norm_gain, project, gate_matrix, out_gain, final_matrix):
    far, near, col_parts = sizes
    row_count, col_count, features = pair_state.shape
    parts = near * col_parts
    width = features // parts
    left_part, right_part, gating = project_in(pair_state, norm_gain, project, gate_matrix)
    both = jnp.stack([left_part.reshape(parts, width, -1), right_part.reshape(parts, width, -1)], axis=1)
    both = lax.all_to_all(both, EVERY, split_axis=0, concat_axis=0, tiled=True)
    both = both.reshape(near, col_parts, 2, width, row_count, col_count)
    both = both.transpose(2, 3, 0, 4, 1, 5).reshape(2, width, near * row_count, col_parts * col_count)
    left_part, right_part = both[0], both[1]
    if incoming:
        mixture = jnp.einsum("cki,ckj->cij", left_part, right_part, preferred_element_type=jnp.float32)
        if far > 1:
            mixture = lax.psum_scatter(mixture, "far", scatter_dimension=1, tiled=True)
    else:
        if far > 1:
            right_part = lax.all_gather(right_part, "far", axis=1, tiled=True)
        mixture = jnp.einsum("cik,cjk->cij", left_part, right_part, preferred_element_type=jnp.float32)
    mixture = mixture.astype(jnp.bfloat16).reshape(width, near, row_count, col_parts, col_count)
    mixture = mixture.transpose(1, 3, 0, 2, 4).reshape(parts, width, row_count * col_count)
    mixture = lax.all_to_all(mixture, EVERY, split_axis=0, concat_axis=0, tiled=True)
    return finish(pair_state, mixture.reshape(features, -1), gating, out_gain, final_matrix)


def split_rows(row_parts, col_parts, features, least):
    near = row_parts
    while near > 1 and (row_parts % near or features % (near * col_parts) or features < least * near * col_parts):
        near -= 1
    return row_parts // near, near


SMEM_SPEC = pl.BlockSpec(memory_space=pltpu.SMEM)
VMEM_SPEC = pl.BlockSpec(memory_space=pltpu.VMEM)


def lane_norm(values, norm_gain):
    lanes = values.shape[1]
    mean = jnp.dot(values, jnp.full((lanes, lanes), 1 / lanes, jnp.bfloat16), preferred_element_type=jnp.float32)
    centred = values.astype(jnp.float32) - mean
    variance = jnp.mean(centred * centred, axis=1, keepdims=True)
    return centred * lax.rsqrt(variance + epsilon) * norm_gain


def near_core(array):
    return pltpu.with_memory_space_constraint(array, pltpu.VMEM)


def step_lanes(span):
    return pl.ds(pl.multiple_of(pl.program_id(0) * span, span), span)


def emit_projections(normed, rows_ref, out_refs):
    step = normed.shape[0]
    half = rows_ref.shape[0] // 2
    group = 256 if step % 256 == 0 else LANES
    for begin in range(0, step, group):
        projected = lax.dot_general(
            rows_ref[...], normed[begin : begin + group, :], (((1,), (1,)), ((), ())), preferred_element_type=jnp.float32
        )
        gated = sigmoid(projected[:half, :]) * projected[half:, :]
        at = 0
        for ref in out_refs:
            parts, width, _ = ref.shape
            for part in range(parts):
                ref[part, :, begin : begin + group] = gated[at : at + width, :].astype(ref.dtype)
                at += width


def project_kernel(state_ref, gain_ref, rows_ref, *out_refs):
    normed = lane_norm(state_ref[...], gain_ref[...]).astype(jnp.bfloat16)
    emit_projections(normed, rows_ref, out_refs)


def finish_kernel(pieces, onward, *refs):
    mix_refs, refs = refs[:pieces], refs[pieces:]
    state_ref, gain_ref, gate_ref, out_gain_ref, final_ref = refs[:5]
    state = state_ref[...].astype(jnp.float32)
    normed = lane_norm(state_ref[...], gain_ref[...]).astype(jnp.bfloat16)
    gating = sigmoid(jnp.dot(normed, gate_ref[...], preferred_element_type=jnp.float32))
    lanes = step_lanes(state.shape[0])
    mixed = jnp.concatenate(
        [ref[part, :, lanes].astype(jnp.float32) for ref in mix_refs for part in range(ref.shape[0])], axis=0
    )
    mixed = layer_norm(mixed, out_gain_ref[...], 0).astype(jnp.bfloat16)
    change = lax.dot_general(
        mixed, final_ref[...], (((0,), (0,)), ((), ())), preferred_element_type=jnp.float32
    )
    result = (state + gating * change).astype(jnp.bfloat16)
    if onward:
        next_gain, rows_ref, middle_ref = refs[5:8]
        middle_ref[...] = result
        normed = lane_norm(result, next_gain[...]).astype(jnp.bfloat16)
        emit_projections(normed, rows_ref, refs[8:])
    else:
        refs[5][...] = result


def whole_spec(array):
    return pl.BlockSpec(array.shape, lambda step: (0,) * array.ndim)


def row_step(positions):
    step = positions
    for candidate in range(LANES, 2304 + 1, LANES):
        if positions % candidate == 0:
            step = candidate
    return step


def run_projections(state, gain, rows, out_shapes):
    positions, features = state.shape
    step = row_step(positions)
    weights = (gain[None, :], rows)
    return pl.pallas_call(
        project_kernel,
        grid=(positions // step,),
        in_specs=[pl.BlockSpec((step, features), lambda i: (i, 0))] + [whole_spec(w) for w in weights],
        out_specs=[pl.BlockSpec((*shape, step), lambda i: (0, 0, i)) for shape in out_shapes],
        out_shape=[jax.ShapeDtypeStruct((*shape, positions), jnp.bfloat16) for shape in out_shapes],
        compiler_params=pltpu.CompilerParams(vmem_limit_bytes=BUDGET),
        name="project",
    )(state, *weights)


def run_finish(mixes, state, gain, gate_matrix, out_gain, final_matrix, onward=None):
    positions, features = state.shape
    step = row_step(positions)
    weights = (gain[None, :], gate_matrix, out_gain[:, None], final_matrix)
    out_shape = [jax.ShapeDtypeStruct((positions, features), jnp.bfloat16)]
    out_specs = [pl.BlockSpec((step, features), lambda i: (i, 0))]
    if onward is not None:
        next_gain, rows, out_shapes = onward
        weights += (next_gain[None, :], rows)
        out_shape += [jax.ShapeDtypeStruct((*shape, positions), jnp.bfloat16) for shape in out_shapes]
        out_specs += [pl.BlockSpec((*shape, step), lambda i: (0, 0, i)) for shape in out_shapes]
    return pl.pallas_call(
        functools.partial(finish_kernel, len(mixes), onward is not None),
        grid=(positions // step,),
        in_specs=[VMEM_SPEC] * len(mixes)
        + [pl.BlockSpec((step, features), lambda i: (i, 0))]
        + [whole_spec(w) for w in weights],
        out_specs=out_specs,
        out_shape=out_shape,
        compiler_params=pltpu.CompilerParams(vmem_limit_bytes=BUDGET),
        name="finish",
    )(*map(near_core, mixes), state, *weights)


class Folds:
    def __init__(self, row_count, col_count):
        turn = 1
        while (turn * col_count) % LANES:
            turn *= 2
        self.turn, self.tiles = turn, turn * col_count // LANES
        self.cols, self.rows = col_count, row_count
        self.groups = row_count // turn
        self.lane_rows = row_count * col_count // LANES

    def fits(self):
        return self.cols <= LANES and self.rows % self.turn == 0 and self.groups % 8 == 0

    def split(self, lane_rows, clear=False):
        lane = lax.broadcasted_iota(jnp.int32, lane_rows[0].shape, 1)
        out = []
        for phase in range(self.turn):
            first, offset = divmod(phase * self.cols, LANES)
            value = lane_rows[first]
            if offset + self.cols > LANES:
                value = jnp.where(lane >= offset, value, lane_rows[first + 1])
            if offset:
                value = pltpu.roll(value, LANES - offset, 1)
            out.append(jnp.where(lane < self.cols, value, 0.0) if clear else value)
        return out

    def join(self, block_rows):
        lane = lax.broadcasted_iota(jnp.int32, block_rows[0].shape, 1)
        rolled = []
        for phase, value in enumerate(block_rows):
            offset = (phase * self.cols) % LANES
            rolled.append(pltpu.roll(value, offset, 1) if offset else value)
        out = []
        for tile in range(self.tiles):
            value = None
            for phase in range(self.turn):
                begin, end = phase * self.cols - tile * LANES, (phase + 1) * self.cols - tile * LANES
                if end <= 0 or begin >= LANES:
                    continue
                value = rolled[phase] if value is None else jnp.where(lane >= begin, rolled[phase], value)
            out.append(value)
        return out


def stage(source_ref, staged):
    parts, width, positions = source_ref.shape
    rows = parts * width

    @pl.loop(0, positions // LANES, unroll=8)
    def _(tile):
        lanes = pl.ds(pl.multiple_of(tile * LANES, LANES), LANES)
        for part in range(parts):
            staged[pl.ds(tile * rows + part * width, width), :] = source_ref[part, :, lanes].astype(jnp.float32)


def unstage(staged, target_ref, earlier_refs=()):
    parts, height, positions = target_ref.shape
    width = height - sum(ref.shape[1] for ref in earlier_refs)
    rows = parts * width

    @pl.loop(0, positions // LANES, unroll=8)
    def _(tile):
        lanes = pl.ds(pl.multiple_of(tile * LANES, LANES), LANES)
        for part in range(parts):
            values = [ref[part, :, lanes].astype(jnp.float32) for ref in earlier_refs]
            values.append(staged[pl.ds(tile * rows + part * width, width), :])
            values = values[0] if len(values) == 1 else jnp.concatenate(values, axis=0)
            target_ref[part, :, lanes] = values.astype(target_ref.dtype)


def lane_rows_of(folds, rows, row):
    return [pl.ds(row + tile * rows, folds.groups, stride=folds.tiles * rows) for tile in range(folds.tiles)]


def mix_out_kernel(folds, near, cols, width, stages, half_ref, *refs):
    parts = near * cols
    rows = parts * width
    block = folds.rows
    tall = near * block
    earlier_refs, near_ref = (), None
    if stages == (0, 1):
        left_ref, right_ref, there_ref, *earlier_refs, mix_ref, staged, right, folded, left = refs
    elif stages == (0,):
        left_ref, right_ref, mix_ref, left, staged, right, folded = refs
    else:
        left, near_ref, there_ref, *earlier_refs, mix_ref, staged, right, folded = refs

    def unfold(ref, shift, store):
        height = ref.shape[1]
        stage(ref, staged)

        @pl.loop(0, rows, unroll=8)
        def _(step):
            source, channel = step // width, step % width
            row = source * height + shift + channel
            store(source, channel, [staged[at, :] for at in lane_rows_of(folds, parts * height, row)])

    def store_left(source, channel, lane_rows):
        pieces = folds.split(lane_rows, clear=True)
        at = (channel * cols + source % cols) * tall + (source // cols) * block
        left[pl.ds(pl.multiple_of(at, block), block), :] = jnp.concatenate(pieces, axis=0).astype(jnp.bfloat16)

    def store_right(source, channel, lane_rows):
        at = (channel * cols + source % cols) * tall + (source // cols) * block
        for phase, piece in enumerate(folds.split(lane_rows)):
            right[pl.ds(at + phase, folds.groups, stride=folds.turn), :] = piece

    def products(half):
        @pl.loop(0, width)
        def _(channel):
            starts = [(channel * cols + col) * tall for col in range(cols)]
            lhs = jnp.concatenate([left[pl.ds(pl.multiple_of(at, block), tall), :] for at in starts], axis=1)
            for offset in range(near):
                at = [pl.multiple_of(start + offset * block, block) for start in starts]
                rhs = jnp.concatenate([right[pl.ds(begin, block), :] for begin in at], axis=1).astype(jnp.bfloat16)
                total = lax.dot_general(lhs, rhs, (((1,), (1,)), ((), ())), preferred_element_type=jnp.float32)
                total = jnp.concatenate([total, jnp.zeros((tall, LANES - block), jnp.float32)], axis=1)
                for piece in range(near):
                    lane_rows = folds.join(
                        [
                            total[piece * block + phase * folds.groups : piece * block + (phase + 1) * folds.groups, :]
                            for phase in range(folds.turn)
                        ]
                    )
                    out_row = (piece * cols + half * near + offset) * width + channel
                    for lanes, value in zip(lane_rows_of(folds, rows, out_row), lane_rows):
                        folded[lanes, :] = value

    if 0 in stages:
        unfold(left_ref, 0, store_left)
        unfold(right_ref, right_ref.shape[1] - width, store_right)
        products(half_ref[0])
    if 1 in stages:
        unfold(there_ref, 0, store_right)
        products(half_ref[1])

    @pl.loop(0, mix_ref.shape[2] // LANES, unroll=8)
    def _(tile):
        lanes = pl.ds(pl.multiple_of(tile * LANES, LANES), LANES)
        for part in range(parts):
            value = folded[pl.ds(tile * rows + part * width, width), :]
            if near_ref is not None:
                mine = half_ref[0] == part % cols // near
                value = jnp.where(mine, near_ref[part, :, lanes].astype(jnp.float32), value)
            values = [ref[part, :, lanes].astype(jnp.float32) for ref in earlier_refs] + [value]
            values = values[0] if len(values) == 1 else jnp.concatenate(values, axis=0)
            mix_ref[part, :, lanes] = values.astype(mix_ref.dtype)


def mix_in_kernel(folds, near, cols, width, stages, half_ref, both_ref, *refs):
    targets, (staged, left, right, turned, mixed) = refs[:-5], refs[-5:]
    parts = near * cols
    block = folds.rows
    tall = near * block
    out_rows = parts * width

    stage(both_ref, staged)

    def unfold(target, source, channel, shift):
        row = source * 2 * width + shift + channel
        pieces = folds.split([staged[at, :] for at in lane_rows_of(folds, 2 * out_rows, row)])
        at = (channel * cols + source % cols) * tall + (source // cols) * block
        target[pl.ds(pl.multiple_of(at, block), block), :] = jnp.concatenate(pieces, axis=0).astype(jnp.bfloat16)

    @pl.loop(0, parts * width, unroll=8)
    def _(at):
        unfold(right, at // width, at % width, width)

    for which, target_ref in zip(stages, targets):
        half = half_ref[which]

        @pl.loop(0, near * near * width, unroll=8)
        def _(at):
            place, channel = at // width, at % width
            unfold(left, place // near * cols + half * near + place % near, channel, 0)

        @pl.loop(0, width)
        def _(channel):
            starts = [pl.multiple_of((channel * cols + col) * tall, block) for col in range(cols)]
            rhs = jnp.concatenate([right[pl.ds(start, tall), :] for start in starts], axis=1)
            for piece in range(near):
                start = pl.multiple_of((channel * cols + half * near + piece) * tall, block)
                summed = lax.dot_general(
                    left[pl.ds(start, tall), :], rhs, (((0,), (0,)), ((), ())), preferred_element_type=jnp.float32
                )
                for target in range(cols):
                    turned[piece, target] = summed[:, target * LANES : (target + 1) * LANES]
                    lane_rows = folds.join(
                        [
                            turned[piece, target, pl.ds(phase, folds.groups, stride=folds.turn), :]
                            for phase in range(folds.turn)
                        ]
                    )
                    out_row = (piece * cols + target) * width + channel
                    for lanes, value in zip(lane_rows_of(folds, out_rows, out_row), lane_rows):
                        mixed[lanes, :] = value

        unstage(mixed, target_ref)


def run_mix_out(folds, near, cols, width, stages, halves, *arrays, mine=None, earlier=()):
    parts, _, positions = arrays[-1].shape
    rows = parts * width
    tall = width * cols * near * folds.rows
    out_shape = [jax.ShapeDtypeStruct((parts, width + sum(e.shape[1] for e in earlier), positions), jnp.bfloat16)]
    scratch = [
        pltpu.VMEM((2 * rows * folds.lane_rows, LANES), jnp.float32),
        pltpu.VMEM((tall, LANES), jnp.float32),
        pltpu.VMEM((rows * folds.lane_rows, LANES), jnp.float32),
    ]
    if stages == (0,):
        out_shape.append(jax.ShapeDtypeStruct((tall, LANES), jnp.bfloat16))
    elif stages == (0, 1):
        scratch.append(pltpu.VMEM((tall, LANES), jnp.bfloat16))
    return pl.pallas_call(
        functools.partial(mix_out_kernel, folds, near, cols, width, stages),
        in_specs=[SMEM_SPEC] + [VMEM_SPEC] * (len(arrays) + len(earlier)),
        out_specs=[VMEM_SPEC] * len(out_shape),
        out_shape=out_shape,
        scratch_shapes=scratch,
        compiler_params=pltpu.CompilerParams(vmem_limit_bytes=BUDGET),
        name="mix_out",
    )(halves, *(array if array.ndim < 3 or array is mine else near_core(array) for array in arrays), *earlier)


def add_kernel(*refs):
    target_ref = refs[-1]
    parts = target_ref.shape[0]
    lanes = step_lanes(target_ref.shape[2])
    for part in range(parts):
        sums = [kept[part] + got[part, :, lanes].astype(jnp.float32) for kept, got in zip(refs[:-1:2], refs[1:-1:2])]
        target_ref[part] = jnp.concatenate(sums, axis=0).astype(target_ref.dtype)


def run_add(*arrays):
    parts, _, positions = arrays[0].shape
    step = positions // 2 if positions % (2 * LANES) == 0 else positions
    height = sum(array.shape[1] for array in arrays) // 2
    return pl.pallas_call(
        add_kernel,
        grid=(positions // step,),
        in_specs=[pl.BlockSpec((*array.shape[:2], step), lambda i: (0, 0, i)) if at % 2 == 0 else VMEM_SPEC for at, array in enumerate(arrays)],
        out_specs=pl.BlockSpec((parts, height, step), lambda i: (0, 0, i)),
        out_shape=jax.ShapeDtypeStruct((parts, height, positions), jnp.bfloat16),
        compiler_params=pltpu.CompilerParams(vmem_limit_bytes=BUDGET),
        name="add",
    )(*(near_core(array) if at % 2 else array for at, array in enumerate(arrays)))


def run_mix_in(folds, near, cols, stages, halves, both):
    parts, width, positions = both.shape
    rows, width = parts * width, width // 2
    tall = width * cols * near * folds.rows
    types = (jnp.float32, jnp.bfloat16)
    return pl.pallas_call(
        functools.partial(mix_in_kernel, folds, near, cols, width, stages),
        in_specs=[SMEM_SPEC, VMEM_SPEC],
        out_specs=[VMEM_SPEC] * len(stages),
        out_shape=[jax.ShapeDtypeStruct((parts, width, positions), types[which]) for which in stages],
        scratch_shapes=[
            pltpu.VMEM((rows * folds.lane_rows, LANES), jnp.float32),
            pltpu.VMEM((tall, LANES), jnp.bfloat16),
            pltpu.VMEM((tall, LANES), jnp.bfloat16),
            pltpu.VMEM((near, cols, LANES, LANES), jnp.float32),
            pltpu.VMEM((rows // 2 * folds.lane_rows, LANES), jnp.float32),
        ],
        compiler_params=pltpu.CompilerParams(vmem_limit_bytes=BUDGET),
        name="mix_in",
    )(halves, near_core(both))


SHARES = (1, 1, 1, 1)
GROUPS = ((0, 1), (2, 3))
PIECES = len(SHARES)


def exchange(array):
    return lax.all_to_all(array, EVERY, split_axis=0, concat_axis=0, tiled=True)


def across(array):
    return lax.ppermute(array, "far", ((0, 1), (1, 0)))


def in_halves(sizes, pair_input, weights):
    _, near, cols = sizes
    row_count, col_count, features = pair_input.shape
    parts = near * cols
    width = features // parts
    ends = [sum(SHARES[: at + 1]) * width // sum(SHARES) for at in range(PIECES)]
    begins = [0] + ends[:-1]
    folds = Folds(row_count, col_count)
    half = lax.axis_index("far")
    halves = jnp.stack([half, 1 - half]).astype(jnp.int32)

    def rows_of(project, *arrays):
        ga, va, gb, vb = (rows.reshape(parts, width, features) for rows in jnp.split(project.T, 4, axis=0))

        def ordered(left, right):
            return [
                jnp.concatenate(
                    [rows[:, begins[piece] : ends[piece]] for rows, piece in zip((left, right), pair) if piece is not None],
                    axis=1,
                ).reshape(-1, features)
                for pair in arrays
            ]

        return jnp.concatenate(ordered(ga, gb) + ordered(va, vb))

    def shapes_of(*arrays):
        return [
            (parts, sum(ends[piece] - begins[piece] for piece in pair if piece is not None)) for pair in arrays
        ]

    def in_groups(array):
        rows = array.reshape(parts, width, -1)
        ordered = [
            jnp.concatenate([rows[:, begins[piece] : ends[piece]] for piece in group], axis=1).reshape(-1, rows.shape[-1])
            for group in GROUPS
        ]
        return jnp.concatenate(ordered).reshape(array.shape)

    gain_1, project_1, gate_1, norm_1, final_1, gain_2, project_2, gate_2, norm_2, final_2 = weights
    state = pair_input.reshape(-1, features)

    ahead = [(None, 0)] + [(piece, piece + 1) for piece in range(PIECES - 1)] + [(PIECES - 1, None)]
    level = [(piece, piece) for piece in range(PIECES)]
    sent, mixed, mixes = [], [None] * PIECES, []
    out = run_projections(state, gain_1, rows_of(project_1, *ahead[:1]), shapes_of(*ahead[:1]))
    out += run_projections(state, gain_1, rows_of(project_1, *ahead[1:]), shapes_of(*ahead[1:]))
    for array in out:
        sent.append(exchange(array))
    for piece in range(PIECES):
        group = next(group for group in GROUPS if piece in group)
        right, left = sent[piece], sent[piece + 1]
        there = across(right[:, right.shape[1] - (ends[piece] - begins[piece]) :, :])
        earlier = [mixed[other] for other in group[:-1]] if piece == group[-1] else ()
        mix = functools.partial(run_mix_out, folds, near, cols, ends[piece] - begins[piece])
        if piece < PIECES - 1:
            mixed[piece] = mix((0, 1), halves, left, right, there, earlier=earlier)[0]
        else:
            mine, unfolded = mix((0,), halves, left, right)
            mixed[piece] = mix((1,), halves, unfolded, mine, there, mine=mine, earlier=earlier)[0]
        if piece == group[-1]:
            mixes.append(exchange(mixed[piece]))
    onward = (gain_2, rows_of(project_2, *level[:1]), shapes_of(*level[:1]))
    middle, *out = run_finish(mixes, state, gain_1, gate_1, in_groups(norm_1), in_groups(final_1), onward)
    out += run_projections(middle, gain_2, rows_of(project_2, *level[1:]), shapes_of(*level[1:]))
    both, parted, mixes = [], [], []
    for piece in range(PIECES):
        both.append(exchange(out[piece]))
    for piece in range(PIECES):
        mix = functools.partial(run_mix_in, folds, near, cols)
        sent = mix((1,), halves, both[piece])[0]
        kept = mix((0,), halves, both[piece])[0]
        parted.append((kept, across(sent)))
    for group in GROUPS:
        summed = run_add(*(array for piece in group for array in parted[piece]))
        mixes.append(exchange(summed))
    result = run_finish(mixes, middle, gain_2, gate_2, in_groups(norm_2), in_groups(final_2))[0]
    return result.reshape(pair_input.shape)


def solution(mesh):
    row_parts, col_parts = mesh.shape["dap"], mesh.shape["chan"] * mesh.shape["sub"]

    def whole(pair_input, *weights):
        features = pair_input.shape[-1]
        block_rows = pair_input.shape[0] // (mesh.shape["groups"] * row_parts)
        block_cols = pair_input.shape[1] // col_parts
        halved = (
            row_parts % 2 == 0
            and row_parts == col_parts
            and block_rows == block_cols
            and Folds(block_rows, block_cols).fits()
            and features == LANES
            and features % (row_parts // 2 * col_parts * sum(SHARES)) == 0
        )
        if halved:
            far, near = 2, row_parts // 2
        else:
            far, near = split_rows(row_parts, col_parts, features, 8)
        sizes = (far, near, col_parts)
        finer = Mesh(
            mesh.devices.reshape(mesh.shape["groups"], far, near, mesh.shape["chan"], mesh.shape["sub"]),
            ("groups", "far", "near", "chan", "sub"),
        )

        def shards(pair_input, *weights):
            if halved:
                return in_halves(sizes, pair_input, weights)
            middle = update(False, sizes, pair_input, *weights[:5])
            return update(True, sizes, middle, *weights[5:])

        pair_spec = P(("groups", "far", "near"), ("chan", "sub"), None)
        mapped = jax.shard_map(
            shards,
            mesh=finer,
            in_specs=(pair_spec,) + (P(),) * 10,
            out_specs=pair_spec,
            check_vma=False,
        )
        return mapped(pair_input, *weights)

    return whole
```

profile of v0, /device:TPU:0, one launch (start us, length us, event | category | flops | bytes accessed | tf_op | source)
XLA Modules:
  0.0 458.3 jit_solution(884853186412215360)
XLA Ops:
  12.9 6.8 %project.3 = (bf16[8,8,9216]{2,1,0:T(8,128)(2,1)}, bf16[8,8,9216]{2,1,0:T(8,128)(2,1)}, bf16[8,8,9216]{2,1,0:T(8,128)(2,1)}, bf16[8,4,9216]{2,1,0:T(4,128)(2,1)}) custom-call(bf16[9216,128]{1,0:T(8,128)(2,1)} %bitcast.91, f32[1,128]{1,0:T(1,128)} %bitcast.110, bf16[448,128]{1,0:T(8,128)(2,1)} %copy-done.7), custom_call_target="tpu_custom_call" | custom-call | tf_op jit(solution)/shard_map/project/pallas_call | solution.py:163
  21.7 14.5 %all_to_all.65.refs_0_ = bf16[8,4,9216]{2,1,0:T(4,128)(2,1)} all-to-all(bf16[8,4,9216]{2,1,0:T(4,128)(2,1)} %get-tuple-element.18), channel_id=1, replica_groups=mesh['groups'=2,'far'=2,'near'=2,'chan'=2,'sub'=2] {'near','chan','sub'}, dimensions={0} | all-to-all | bytes 1179648 | tf_op jit(solution)/shard_map/all_to_all | solution.py:475
  36.2 19.1 %all_to_all.66.refs_0_.refs_1_ = bf16[8,8,9216]{2,1,0:T(8,128)(2,1)S(1)} all-to-all(bf16[8,8,9216]{2,1,0:T(8,128)(2,1)S(1)} %copy-done.5), channel_id=1, replica_groups=mesh['groups'=2,'far'=2,'near'=2,'chan'=2,'sub'=2] {'near','chan','sub'}, dimensions={0} | all-to-all | bytes 2359296 | tf_op jit(solution)/shard_map/all_to_all | solution.py:475
  55.3 18.9 %all_to_all.67.refs_0_.refs_1_ = bf16[8,8,9216]{2,1,0:T(8,128)(2,1)S(1)} all-to-all(bf16[8,8,9216]{2,1,0:T(8,128)(2,1)S(1)} %copy-done.4), channel_id=1, replica_groups=mesh['groups'=2,'far'=2,'near'=2,'chan'=2,'sub'=2] {'near','chan','sub'}, dimensions={0} | all-to-all | bytes 2359296 | tf_op jit(solution)/shard_map/all_to_all | solution.py:475
  82.6 21.9 %collective-permute-done.1.refs_2_ = bf16[8,4,9216]{2,1,0:T(4,128)(2,1)} collective-permute-done((bf16[8,4,9216]{2,1,0:T(4,128)(2,1)}, bf16[8,4,9216]{2,1,0:T(4,128)(2,1)}, u32[]{:S(2)}, u32[]{:S(2)}) %collective-permute-start.1) | collective-permute-done | bytes 589856 | tf_op jit(solution)/shard_map/ppermute | solution.py:479
  105.6 10.6 %mix_out.5.refs_3_ = bf16[8,4,9216]{2,1,0:T(4,128)(2,1)} custom-call(s32[2]{0:T(128)} %pad_add_fusion.half_ref, bf16[8,8,9216]{2,1,0:T(8,128)(2,1)S(1)} %all_to_all.67.refs_0_.refs_1_, bf16[8,4,9216]{2,1,0:T(4,128)(2,1)S(1)} %copy-done.2, bf16[8,4,9216]{2,1,0:T(4,128)(2,1)} %collective-permute-done.1.refs_2_), custom_call_target="tpu_custom_call" | custom-call | tf_op jit(solution)/shard_map/mix_out/pallas_call | solution.py:412
  116.1 16.5 %collective-permute-done.refs_2_ = bf16[8,4,9216]{2,1,0:T(4,128)(2,1)} collective-permute-done((bf16[8,4,9216]{2,1,0:T(4,128)(2,1)}, bf16[8,4,9216]{2,1,0:T(4,128)(2,1)}, u32[]{:S(2)}, u32[]{:S(2)}) %collective-permute-start) | collective-permute-done | bytes 589856 | tf_op jit(solution)/shard_map/ppermute | solution.py:479
  132.6 11.4 %mix_out.6 = bf16[8,8,9216]{2,1,0:T(8,128)(2,1)} custom-call(s32[2]{0:T(128)} %pad_add_fusion.half_ref, bf16[8,8,9216]{2,1,0:T(8,128)(2,1)S(1)} %all_to_all.66.refs_0_.refs_1_, bf16[8,8,9216]{2,1,0:T(8,128)(2,1)S(1)} %all_to_all.67.refs_0_.refs_1_, bf16[8,4,9216]{2,1,0:T(4,128)(2,1)} %collective-permute-done.refs_2_, bf16[8,4,9216]{2,1,0:T(4,128)(2,1)} %mix_out.5.refs_3_), custom_call_target="tpu_custom_call" | custom-call | tf_op jit(solution)/shard_map/mix_out/pallas_call | solution.py:412
  151.2 7.1 %mix_out.7 = (bf16[8,4,9216]{2,1,0:T(4,128)(2,1)}, bf16[3072,128]{1,0:T(8,128)(2,1)}) custom-call(s32[2]{0:T(128)} %pad_add_fusion.half_ref, bf16[8,4,9216]{2,1,0:T(4,128)(2,1)S(1)} %copy-done.3, bf16[8,8,9216]{2,1,0:T(8,128)(2,1)S(1)} %all-to-all-done.5.refs_1_.refs_0_), custom_call_target="tpu_custom_call" | custom-call | tf_op jit(solution)/shard_map/mix_out/pallas_call | solution.py:412
  158.4 15.8 %collective-permute-done.3.refs_2_ = bf16[8,4,9216]{2,1,0:T(4,128)(2,1)S(1)} collective-permute-done((bf16[8,4,9216]{2,1,0:T(4,128)(2,1)S(1)}, bf16[8,4,9216]{2,1,0:T(4,128)(2,1)S(1)}, u32[]{:S(2)}, u32[]{:S(2)}) %collective-permute-start.3) | collective-permute-done | bytes 589856 | tf_op jit(solution)/shard_map/ppermute | solution.py:479
  174.2 10.3 %mix_out.8.refs_3_ = bf16[8,4,9216]{2,1,0:T(4,128)(2,1)} custom-call(s32[2]{0:T(128)} %pad_add_fusion.half_ref, bf16[8,8,9216]{2,1,0:T(8,128)(2,1)S(1)} %all-to-all-done.5.refs_1_.refs_0_, bf16[8,8,9216]{2,1,0:T(8,128)(2,1)S(1)} %all_to_all.66.refs_0_.refs_1_, bf16[8,4,9216]{2,1,0:T(4,128)(2,1)S(1)} %collective-permute-done.3.refs_2_), custom_call_target="tpu_custom_call" | custom-call | tf_op jit(solution)/shard_map/mix_out/pallas_call | solution.py:412
  184.5 18.3 %collective-permute-done.2.refs_2_ = bf16[8,4,9216]{2,1,0:T(4,128)(2,1)S(1)} collective-permute-done((bf16[8,4,9216]{2,1,0:T(4,128)(2,1)S(1)}, bf16[8,4,9216]{2,1,0:T(4,128)(2,1)S(1)}, u32[]{:S(2)}, u32[]{:S(2)}) %collective-permute-start.2) | collective-permute-done | bytes 589856 | tf_op jit(solution)/shard_map/ppermute | solution.py:479
  202.7 6.5 %mix_out.9 = bf16[8,8,9216]{2,1,0:T(8,128)(2,1)} custom-call(s32[2]{0:T(128)} %pad_add_fusion.half_ref, bf16[3072,128]{1,0:T(8,128)(2,1)} %get-tuple-element.20.refs_0_, bf16[8,4,9216]{2,1,0:T(4,128)(2,1)} %get-tuple-element.21.refs_1_, bf16[8,4,9216]{2,1,0:T(4,128)(2,1)S(1)} %collective-permute-done.2.refs_2_, bf16[8,4,9216]{2,1,0:T(4,128)(2,1)} %mix_out.8.refs_3_), custom_call_target="tpu_custom_call" | custom-call | tf_op jit(solution)/shard_map/mix_out/pallas_call | solution.py:412
  215.8 13.0 %all-to-all-done.6.refs_1_ = bf16[8,8,9216]{2,1,0:T(8,128)(2,1)S(1)} async-done(((bf16[8,8,9216]{2,1,0:T(8,128)(2,1)}), bf16[8,8,9216]{2,1,0:T(8,128)(2,1)S(1)}, u32[]{:S(2)}, u32[]{:S(2)}) %all-to-all-start.6) | async-done | bytes 1179680 | tf_op jit(solution)/shard_map/all_to_all | solution.py:475
  228.8 8.5 %finish.2 = (bf16[9216,128]{1,0:T(8,128)(2,1)}, bf16[8,8,9216]{2,1,0:T(8,128)(2,1)}) custom-call(bf16[8,8,9216]{2,1,0:T(8,128)(2,1)S(1)} %all-to-all-done.3.refs_0_, bf16[8,8,9216]{2,1,0:T(8,128)(2,1)S(1)} %all-to-all-done.6.refs_1_, bf16[9216,128]{1,0:T(8,128)(2,1)} %bitcast.92, f32[1,128]{1,0:T(1,128)} %bitcast.111, bf16[128,128]{1,0:T(8,128)(2,1)} %refs_4_.2, ...), custom_call_target="tpu_custom_call" | custom-call | tf_op jit(solution)/shard_map/finish/pallas_call | solution.py:185
  241.6 6.5 %project.5 = (bf16[8,8,9216]{2,1,0:T(8,128)(2,1)}, bf16[8,8,9216]{2,1,0:T(8,128)(2,1)}, bf16[8,8,9216]{2,1,0:T(8,128)(2,1)}) custom-call(bf16[9216,128]{1,0:T(8,128)(2,1)} %get-tuple-element.23.state_ref.refs_2_, f32[1,128]{1,0:T(1,128)} %bitcast.113, bf16[384,128]{1,0:T(8,128)(2,1)} %copy-done.8), custom_call_target="tpu_custom_call" | custom-call | tf_op jit(solution)/shard_map/project/pallas_call | solution.py:163
  248.1 8.5 %all-to-all-done.7.both_ref = bf16[8,8,9216]{2,1,0:T(8,128)(2,1)S(1)} async-done(((bf16[8,8,9216]{2,1,0:T(8,128)(2,1)}), bf16[8,8,9216]{2,1,0:T(8,128)(2,1)S(1)}, u32[]{:S(2)}, u32[]{:S(2)}) %all-to-all-start.7) | async-done | bytes 1179680 | tf_op jit(solution)/shard_map/all_to_all | solution.py:475
  256.6 20.9 %all_to_all.68.both_ref = bf16[8,8,9216]{2,1,0:T(8,128)(2,1)} all-to-all(bf16[8,8,9216]{2,1,0:T(8,128)(2,1)} %get-tuple-element.24), channel_id=1, replica_groups=mesh['groups'=2,'far'=2,'near'=2,'chan'=2,'sub'=2] {'near','chan','sub'}, dimensions={0} | all-to-all | bytes 2359296 | tf_op jit(solution)/shard_map/all_to_all | solution.py:475
  277.6 18.9 %all_to_all.69.both_ref = bf16[8,8,9216]{2,1,0:T(8,128)(2,1)S(1)} all-to-all(bf16[8,8,9216]{2,1,0:T(8,128)(2,1)S(1)} %copy-done.6), channel_id=1, replica_groups=mesh['groups'=2,'far'=2,'near'=2,'chan'=2,'sub'=2] {'near','chan','sub'}, dimensions={0} | all-to-all | bytes 2359296 | tf_op jit(solution)/shard_map/all_to_all | solution.py:475
  300.1 6.6 %mix_in.9 = bf16[8,4,9216]{2,1,0:T(4,128)(2,1)} custom-call(s32[2]{0:T(128)} %pad_add_fusion.half_ref, bf16[8,8,9216]{2,1,0:T(8,128)(2,1)S(1)} %all-to-all-done.7.both_ref), custom_call_target="tpu_custom_call" | custom-call | tf_op jit(solution)/shard_map/mix_in/pallas_call | solution.py:452
  309.6 6.4 %mix_in.11 = bf16[8,4,9216]{2,1,0:T(4,128)(2,1)} custom-call(s32[2]{0:T(128)} %pad_add_fusion.half_ref, bf16[8,8,9216]{2,1,0:T(8,128)(2,1)S(1)} %copy-done), custom_call_target="tpu_custom_call" | custom-call | tf_op jit(solution)/shard_map/mix_in/pallas_call | solution.py:452
  316.0 6.6 %mix_in.8.refs_0_ = f32[8,4,9216]{2,1,0:T(4,128)} custom-call(s32[2]{0:T(128)} %pad_add_fusion.half_ref, bf16[8,8,9216]{2,1,0:T(8,128)(2,1)S(1)} %all-to-all-done.7.both_ref), custom_call_target="tpu_custom_call" | custom-call | tf_op jit(solution)/shard_map/mix_in/pallas_call | solution.py:452
  322.6 6.6 %mix_in.10.refs_2_ = f32[8,4,9216]{2,1,0:T(4,128)} custom-call(s32[2]{0:T(128)} %pad_add_fusion.half_ref, bf16[8,8,9216]{2,1,0:T(8,128)(2,1)S(1)} %copy-done), custom_call_target="tpu_custom_call" | custom-call | tf_op jit(solution)/shard_map/mix_in/pallas_call | solution.py:452
  329.2 20.1 %collective-permute-done.4.refs_1_ = bf16[8,4,9216]{2,1,0:T(4,128)(2,1)S(1)} collective-permute-done((bf16[8,4,9216]{2,1,0:T(4,128)(2,1)}, bf16[8,4,9216]{2,1,0:T(4,128)(2,1)S(1)}, u32[]{:S(2)}, u32[]{:S(2)}) %collective-permute-start.4) | collective-permute-done | bytes 589856 | tf_op jit(solution)/shard_map/ppermute | solution.py:479
  349.3 12.3 %collective-permute-done.5.refs_3_ = bf16[8,4,9216]{2,1,0:T(4,128)(2,1)S(1)} collective-permute-done((bf16[8,4,9216]{2,1,0:T(4,128)(2,1)}, bf16[8,4,9216]{2,1,0:T(4,128)(2,1)S(1)}, u32[]{:S(2)}, u32[]{:S(2)}) %collective-permute-start.5) | collective-permute-done | bytes 589856 | tf_op jit(solution)/shard_map/ppermute | solution.py:479
  368.1 6.4 %mix_in.13 = bf16[8,4,9216]{2,1,0:T(4,128)(2,1)} custom-call(s32[2]{0:T(128)} %pad_add_fusion.half_ref, bf16[8,8,9216]{2,1,0:T(8,128)(2,1)S(1)} %all_to_all.69.both_ref), custom_call_target="tpu_custom_call" | custom-call | tf_op jit(solution)/shard_map/mix_in/pallas_call | solution.py:452
  383.8 6.6 %mix_in.12.refs_0_ = f32[8,4,9216]{2,1,0:T(4,128)} custom-call(s32[2]{0:T(128)} %pad_add_fusion.half_ref, bf16[8,8,9216]{2,1,0:T(8,128)(2,1)S(1)} %all_to_all.69.both_ref), custom_call_target="tpu_custom_call" | custom-call | tf_op jit(solution)/shard_map/mix_in/pallas_call | solution.py:452
  390.4 6.6 %mix_in.14.refs_2_ = f32[8,4,9216]{2,1,0:T(4,128)} custom-call(s32[2]{0:T(128)} %pad_add_fusion.half_ref, bf16[8,8,9216]{2,1,0:T(8,128)(2,1)S(1)} %all-to-all-done.11.both_ref), custom_call_target="tpu_custom_call" | custom-call | tf_op jit(solution)/shard_map/mix_in/pallas_call | solution.py:452
  397.1 20.1 %collective-permute-done.6.refs_1_ = bf16[8,4,9216]{2,1,0:T(4,128)(2,1)S(1)} collective-permute-done((bf16[8,4,9216]{2,1,0:T(4,128)(2,1)}, bf16[8,4,9216]{2,1,0:T(4,128)(2,1)S(1)}, u32[]{:S(2)}, u32[]{:S(2)}) %collective-permute-start.6) | collective-permute-done | bytes 589856 | tf_op jit(solution)/shard_map/ppermute | solution.py:479
  417.1 12.2 %collective-permute-done.7.refs_3_ = bf16[8,4,9216]{2,1,0:T(4,128)(2,1)S(1)} collective-permute-done((bf16[8,4,9216]{2,1,0:T(4,128)(2,1)}, bf16[8,4,9216]{2,1,0:T(4,128)(2,1)S(1)}, u32[]{:S(2)}, u32[]{:S(2)}) %collective-permute-start.7) | collective-permute-done | bytes 589856 | tf_op jit(solution)/shard_map/ppermute | solution.py:479
  437.5 14.0 %all-to-all-done.12.refs_1_ = bf16[8,8,9216]{2,1,0:T(8,128)(2,1)S(1)} async-done(((bf16[8,8,9216]{2,1,0:T(8,128)(2,1)}), bf16[8,8,9216]{2,1,0:T(8,128)(2,1)S(1)}, u32[]{:S(2)}, u32[]{:S(2)}) %all-to-all-start.12) | async-done | bytes 1179680 | tf_op jit(solution)/shard_map/all_to_all | solution.py:475
  451.5 6.7 %finish.3 = bf16[9216,128]{1,0:T(8,128)(2,1)} custom-call(bf16[8,8,9216]{2,1,0:T(8,128)(2,1)S(1)} %all-to-all-done.9.refs_0_, bf16[8,8,9216]{2,1,0:T(8,128)(2,1)S(1)} %all-to-all-done.12.refs_1_, bf16[9216,128]{1,0:T(8,128)(2,1)} %get-tuple-element.23.state_ref.refs_2_, f32[1,128]{1,0:T(1,128)} %bitcast.114, bf16[128,128]{1,0:T(8,128)(2,1)} %refs_4_.3, ...), custom_call_target="tpu_custom_call" | custom-call | tf_op jit(solution)/shard_map/finish/pallas_call | solution.py:185
  (99 shorter events, 72.7 us)
Async XLA Ops:
  6.9 14.8 %all-to-all-start.2 = ((bf16[8,4,9216]{2,1,0:T(4,128)(2,1)}), bf16[8,4,9216]{2,1,0:T(4,128)(2,1)S(1)}, u32[]{:S(2)}, u32[]{:S(2)}) async-start(bf16[8,4,9216]{2,1,0:T(4,128)(2,1)} %project.4), calls=%async_computation.2 | async-start | bytes 1179648 | tf_op jit(solution)/shard_map/all_to_all | solution.py:475
  12.3 0.6 copy-start.7
  19.7 16.5 %copy-start.5 = (bf16[8,8,9216]{2,1,0:T(8,128)(2,1)S(1)}, bf16[8,8,9216]{2,1,0:T(8,128)(2,1)}, u32[]{:S(2)}) copy-start(bf16[8,8,9216]{2,1,0:T(8,128)(2,1)} %get-tuple-element.16) | copy-start | bytes 3538948
  21.7 33.6 %copy-start.1 = (bf16[8,4,9216]{2,1,0:T(4,128)(2,1)}, bf16[8,4,9216]{2,1,0:T(4,128)(2,1)S(1)}, u32[]{:S(2)}) copy-start(bf16[8,4,9216]{2,1,0:T(4,128)(2,1)S(1)} %all-to-all-done.2.refs_1_) | copy-start | bytes 1769476
  36.2 19.1 %copy-start.4 = (bf16[8,8,9216]{2,1,0:T(8,128)(2,1)S(1)}, bf16[8,8,9216]{2,1,0:T(8,128)(2,1)}, u32[]{:S(2)}) copy-start(bf16[8,8,9216]{2,1,0:T(8,128)(2,1)} %get-tuple-element.17) | copy-start | bytes 3538948
  74.2 69.7 %all-to-all-start.5 = ((bf16[8,8,9216]{2,1,0:T(8,128)(2,1)}), bf16[8,8,9216]{2,1,0:T(8,128)(2,1)S(1)}, u32[]{:S(2)}, u32[]{:S(2)}) async-start(bf16[8,8,9216]{2,1,0:T(8,128)(2,1)} %get-tuple-element.19), calls=%async_computation.5 | async-start | bytes 2359296 | tf_op jit(solution)/shard_map/all_to_all | solution.py:475
  77.8 26.7 %collective-permute-start.1 = (bf16[8,4,9216]{2,1,0:T(4,128)(2,1)}, bf16[8,4,9216]{2,1,0:T(4,128)(2,1)}, u32[]{:S(2)}, u32[]{:S(2)}) collective-permute-start(bf16[8,4,9216]{2,1,0:T(4,128)(2,1)} %copy-done.1), channel_id=1, source_target_pairs={{0,8},{8,0},{1,9},{9,1},{2,10},{10,2},{3,11},{11,3},{4,12},{12,4},... | collective-permute-start | bytes 1769480 | tf_op jit(solution)/shard_map/ppermute | solution.py:479
  81.6 51.0 %collective-permute-start = (bf16[8,4,9216]{2,1,0:T(4,128)(2,1)}, bf16[8,4,9216]{2,1,0:T(4,128)(2,1)}, u32[]{:S(2)}, u32[]{:S(2)}) collective-permute-start(bf16[8,4,9216]{2,1,0:T(4,128)(2,1)} %slice.178), channel_id=1, source_target_pairs={{0,8},{8,0},{1,9},{9,1},{2,10},{10,2},{3,11},{11,3},{4,12},{12,4},... | collective-permute-start | bytes 1769480 | tf_op jit(solution)/shard_map/ppermute | solution.py:479
  104.5 1.1 copy-start.2
  144.0 65.3 %all-to-all-start.3 = ((bf16[8,8,9216]{2,1,0:T(8,128)(2,1)}), bf16[8,8,9216]{2,1,0:T(8,128)(2,1)S(1)}, u32[]{:S(2)}, u32[]{:S(2)}) async-start(bf16[8,8,9216]{2,1,0:T(8,128)(2,1)} %mix_out.6), calls=%async_computation.3 | async-start | bytes 2359296 | tf_op jit(solution)/shard_map/all_to_all | solution.py:475
  147.5 3.7 copy-start.3
  147.9 26.3 %collective-permute-start.3 = (bf16[8,4,9216]{2,1,0:T(4,128)(2,1)S(1)}, bf16[8,4,9216]{2,1,0:T(4,128)(2,1)S(1)}, u32[]{:S(2)}, u32[]{:S(2)}) collective-permute-start(bf16[8,4,9216]{2,1,0:T(4,128)(2,1)S(1)} %slice.182), channel_id=1, source_target_pairs={{0,8},{8,0},{1,9},{9,1},{2,10},{10,2},{3,11},{11,3},{4,12},{12,4},... | collective-permute-start | bytes 1769480 | tf_op jit(solution)/shard_map/ppermute | solution.py:479
  151.1 51.6 %collective-permute-start.2 = (bf16[8,4,9216]{2,1,0:T(4,128)(2,1)S(1)}, bf16[8,4,9216]{2,1,0:T(4,128)(2,1)S(1)}, u32[]{:S(2)}, u32[]{:S(2)}) collective-permute-start(bf16[8,4,9216]{2,1,0:T(4,128)(2,1)S(1)} %slice.181), channel_id=1, source_target_pairs={{0,8},{8,0},{1,9},{9,1},{2,10},{10,2},{3,11},{11,3},{4,12},{12,4},... | collective-permute-start | bytes 1769480 | tf_op jit(solution)/shard_map/ppermute | solution.py:479
  209.2 3.9 copy-start.12
  209.2 5.1 %copy-start.9 = (bf16[128,512]{1,0:T(8,128)(2,1)S(1)}, bf16[128,512]{1,0:T(8,128)(2,1)}, u32[]{:S(2)}) copy-start(bf16[128,512]{1,0:T(8,128)(2,1)} %param.18) | copy-start | bytes 393220
  209.3 5.3 %copy-start.10 = (bf16[128,128]{1,0:T(8,128)(2,1)S(1)}, bf16[128,128]{1,0:T(8,128)(2,1)}, u32[]{:S(2)}) copy-start(bf16[128,128]{1,0:T(8,128)(2,1)} %param.16) | copy-start | bytes 98308
  209.3 19.5 %all-to-all-start.6 = ((bf16[8,8,9216]{2,1,0:T(8,128)(2,1)}), bf16[8,8,9216]{2,1,0:T(8,128)(2,1)S(1)}, u32[]{:S(2)}, u32[]{:S(2)}) async-start(bf16[8,8,9216]{2,1,0:T(8,128)(2,1)} %mix_out.9), calls=%async_computation.6 | async-start | bytes 2359296 | tf_op jit(solution)/shard_map/all_to_all | solution.py:475
  237.3 19.4 %all-to-all-start.7 = ((bf16[8,8,9216]{2,1,0:T(8,128)(2,1)}), bf16[8,8,9216]{2,1,0:T(8,128)(2,1)S(1)}, u32[]{:S(2)}, u32[]{:S(2)}) async-start(bf16[8,8,9216]{2,1,0:T(8,128)(2,1)} %get-tuple-element.22), calls=%async_computation.7 | async-start | bytes 2359296 | tf_op jit(solution)/shard_map/all_to_all | solution.py:475
  241.0 0.6 copy-start.8
  256.6 20.9 %copy-start.6 = (bf16[8,8,9216]{2,1,0:T(8,128)(2,1)S(1)}, bf16[8,8,9216]{2,1,0:T(8,128)(2,1)}, u32[]{:S(2)}) copy-start(bf16[8,8,9216]{2,1,0:T(8,128)(2,1)} %get-tuple-element.25) | copy-start | bytes 3538948
  296.5 67.8 %all-to-all-start.11 = ((bf16[8,8,9216]{2,1,0:T(8,128)(2,1)}), bf16[8,8,9216]{2,1,0:T(8,128)(2,1)S(1)}, u32[]{:S(2)}, u32[]{:S(2)}) async-start(bf16[8,8,9216]{2,1,0:T(8,128)(2,1)} %get-tuple-element.26), calls=%async_computation.11 | async-start | bytes 2359296 | tf_op jit(solution)/shard_map/all_to_all | solution.py:475
  300.1 9.5 %copy-start = (bf16[8,8,9216]{2,1,0:T(8,128)(2,1)S(1)}, bf16[8,8,9216]{2,1,0:T(8,128)(2,1)}, u32[]{:S(2)}) copy-start(bf16[8,8,9216]{2,1,0:T(8,128)(2,1)} %all_to_all.68.both_ref) | copy-start | bytes 3538948
  306.6 42.6 %collective-permute-start.4 = (bf16[8,4,9216]{2,1,0:T(4,128)(2,1)}, bf16[8,4,9216]{2,1,0:T(4,128)(2,1)S(1)}, u32[]{:S(2)}, u32[]{:S(2)}) collective-permute-start(bf16[8,4,9216]{2,1,0:T(4,128)(2,1)} %mix_in.9), channel_id=1, source_target_pairs={{0,8},{8,0},{1,9},{9,1},{2,10},{10,2},{3,11},{11,3},{4,12},{12,4},... | collective-permute-start | bytes 1769480 | tf_op jit(solution)/shard_map/ppermute | solution.py:479
  316.0 45.6 %collective-permute-start.5 = (bf16[8,4,9216]{2,1,0:T(4,128)(2,1)}, bf16[8,4,9216]{2,1,0:T(4,128)(2,1)S(1)}, u32[]{:S(2)}, u32[]{:S(2)}) collective-permute-start(bf16[8,4,9216]{2,1,0:T(4,128)(2,1)} %mix_in.11), channel_id=1, source_target_pairs={{0,8},{8,0},{1,9},{9,1},{2,10},{10,2},{3,11},{11,3},{4,12},{12,4},... | collective-permute-start | bytes 1769480 | tf_op jit(solution)/shard_map/ppermute | solution.py:479
  364.3 67.8 %all-to-all-start.9 = ((bf16[8,8,9216]{2,1,0:T(8,128)(2,1)}), bf16[8,8,9216]{2,1,0:T(8,128)(2,1)S(1)}, u32[]{:S(2)}, u32[]{:S(2)}) async-start(bf16[8,8,9216]{2,1,0:T(8,128)(2,1)} %add.4), calls=%async_computation.9 | async-start | bytes 2359296 | tf_op jit(solution)/shard_map/all_to_all | solution.py:475
  374.5 42.6 %collective-permute-start.6 = (bf16[8,4,9216]{2,1,0:T(4,128)(2,1)}, bf16[8,4,9216]{2,1,0:T(4,128)(2,1)S(1)}, u32[]{:S(2)}, u32[]{:S(2)}) collective-permute-start(bf16[8,4,9216]{2,1,0:T(4,128)(2,1)} %mix_in.13), channel_id=1, source_target_pairs={{0,8},{8,0},{1,9},{9,1},{2,10},{10,2},{3,11},{11,3},{4,12},{12,4},... | collective-permute-start | bytes 1769480 | tf_op jit(solution)/shard_map/ppermute | solution.py:479
  383.6 45.8 %collective-permute-start.7 = (bf16[8,4,9216]{2,1,0:T(4,128)(2,1)}, bf16[8,4,9216]{2,1,0:T(4,128)(2,1)S(1)}, u32[]{:S(2)}, u32[]{:S(2)}) collective-permute-start(bf16[8,4,9216]{2,1,0:T(4,128)(2,1)} %mix_in.15), channel_id=1, source_target_pairs={{0,8},{8,0},{1,9},{9,1},{2,10},{10,2},{3,11},{11,3},{4,12},{12,4},... | collective-permute-start | bytes 1769480 | tf_op jit(solution)/shard_map/ppermute | solution.py:479
  432.0 3.7 copy-start.13
  432.0 4.9 %copy-start.11 = (bf16[128,128]{1,0:T(8,128)(2,1)S(1)}, bf16[128,128]{1,0:T(8,128)(2,1)}, u32[]{:S(2)}) copy-start(bf16[128,128]{1,0:T(8,128)(2,1)} %param.21) | copy-start | bytes 98308
  432.0 19.5 %all-to-all-start.12 = ((bf16[8,8,9216]{2,1,0:T(8,128)(2,1)}), bf16[8,8,9216]{2,1,0:T(8,128)(2,1)S(1)}, u32[]{:S(2)}, u32[]{:S(2)}) async-start(bf16[8,8,9216]{2,1,0:T(8,128)(2,1)} %add.5), calls=%async_computation.12 | async-start | bytes 2359296 | tf_op jit(solution)/shard_map/all_to_all | solution.py:475
where the time goes:
time: 460 us; the launch traced here: 458 us
  waiting for transfers between devices  175 us (38%)
  Pallas kernels  137 us (30%)
  blocking collectives  92.4 us (20%)
  starting transfers between devices  42.8 us (9%)
  local copies, waits for them, and re-layouts  7.51 us (2%)
    ppermute x8, waiting for transfers between devices, across(): return lax.ppermute(array, 'far', ((0, 1), (1, 0)))  137 us
    all_to_all x5, blocking collectives, exchange(): return lax.all_to_all(array, EVERY, split_axis=0, concat_axis=0, tiled=True)  92.4 us
    pallas_call x8, Pallas kernels, run_mix_in(): pl.pallas_call(functools.partial(mix_in_kernel, folds, near, cols, width,...  52.3 us
    pallas_call x5, Pallas kernels, run_mix_out(): pl.pallas_call(functools.partial(mix_out_kernel, folds, near, cols, width...  45.9 us
    all_to_all x8, waiting for transfers between devices, exchange(): return lax.all_to_all(array, EVERY, split_axis=0, concat_axis=0, tiled=True)  37.6 us
    all_to_all x8, starting transfers between devices, exchange(): return lax.all_to_all(array, EVERY, split_axis=0, concat_axis=0, tiled=True)  30.9 us
    pallas_call x3, Pallas kernels, run_projections(): pl.pallas_call(project_kernel, grid=(positions // step,), in_specs=[pl.Bl...  18.4 us
    pallas_call x2, Pallas kernels, run_finish(): pl.pallas_call(functools.partial(finish_kernel, len(mixes), onward is not...  15.2 us
  transfers between devices with their start and end apart: 16, of which 12 were waited for; matrix products, arithmetic and copies ran while one was open for 2% of the time, Pallas kernels for 25%

commit v1 on v0

--- a/solution.py
+++ b/solution.py
@@ -467,7 +467,8 @@
 
 
 SHARES = (1, 1, 1, 1)
-GROUPS = ((0, 1), (2, 3))
+OUT_GROUPS = ((0, 1), (2, 3))
+IN_GROUPS = ((0, 1), (2,), (3,))
 PIECES = len(SHARES)
 
 
@@ -509,11 +510,11 @@
             (parts, sum(ends[piece] - begins[piece] for piece in pair if piece is not None)) for pair in arrays
         ]
 
-    def in_groups(array):
+    def in_groups(array, groups):
         rows = array.reshape(parts, width, -1)
         ordered = [
             jnp.concatenate([rows[:, begins[piece] : ends[piece]] for piece in group], axis=1).reshape(-1, rows.shape[-1])
-            for group in GROUPS
+            for group in groups
         ]
         return jnp.concatenate(ordered).reshape(array.shape)
 
@@ -528,7 +529,7 @@
     for array in out:
         sent.append(exchange(array))
     for piece in range(PIECES):
-        group = next(group for group in GROUPS if piece in group)
+        group = next(group for group in OUT_GROUPS if piece in group)
         right, left = sent[piece], sent[piece + 1]
         there = across(right[:, right.shape[1] - (ends[piece] - begins[piece]) :, :])
         earlier = [mixed[other] for other in group[:-1]] if piece == group[-1] else ()
@@ -541,7 +542,7 @@
         if piece == group[-1]:
             mixes.append(exchange(mixed[piece]))
     onward = (gain_2, rows_of(project_2, *level[:1]), shapes_of(*level[:1]))
-    middle, *out = run_finish(mixes, state, gain_1, gate_1, in_groups(norm_1), in_groups(final_1), onward)
+    middle, *out = run_finish(mixes, state, gain_1, gate_1, in_groups(norm_1, OUT_GROUPS), in_groups(final_1, OUT_GROUPS), onward)
     out += run_projections(middle, gain_2, rows_of(project_2, *level[1:]), shapes_of(*level[1:]))
     both, parted, mixes = [], [], []
     for piece in range(PIECES):
@@ -551,10 +552,10 @@
         sent = mix((1,), halves, both[piece])[0]
         kept = mix((0,), halves, both[piece])[0]
         parted.append((kept, across(sent)))
-    for group in GROUPS:
+    for group in IN_GROUPS:
         summed = run_add(*(array for piece in group for array in parted[piece]))
         mixes.append(exchange(summed))
-    result = run_finish(mixes, middle, gain_2, gate_2, in_groups(norm_2), in_groups(final_2))[0]
+    result = run_finish(mixes, middle, gain_2, gate_2, in_groups(norm_2, IN_GROUPS), in_groups(final_2, IN_GROUPS))[0]
     return result.reshape(pair_input.shape)
 
 

time: 460 us -> 487 us (1.059)
  blocking collectives: 92.4 us -> 111 us
    all_to_all x5 -> x6, blocking collectives: 92.4 us -> 111 us  [exchange(): return lax.all_to_all(array, EVERY, split_axis=0, concat_axis=0, tiled=True)]
    all_to_all x8, waiting for transfers between devices: 37.6 us -> 30.8 us  [exchange(): return lax.all_to_all(array, EVERY, split_axis=0, concat_axis=0, tiled=True)]
    ppermute x8, waiting for transfers between devices: 137 us -> 143 us  [across(): return lax.ppermute(array, 'far', ((0, 1), (1, 0)))]
  transfers between devices with their start and end apart: 16 -> 16, of which waited for: 12 -> 11; matrix products, arithmetic and copies ran while one was open for 2% -> 2% of each run, Pallas kernels for 25% -> 23%
where the time goes in v1:
time: 487 us; the launch traced here: 485 us
  waiting for transfers between devices  174 us (36%)
  Pallas kernels  139 us (29%)
  blocking collectives  111 us (23%)
  starting transfers between devices  45.6 us (9%)
  local copies, waits for them, and re-layouts  11 us (2%)
    ppermute x8, waiting for transfers between devices, across(): return lax.ppermute(array, 'far', ((0, 1), (1, 0)))  143 us
    all_to_all x6, blocking collectives, exchange(): return lax.all_to_all(array, EVERY, split_axis=0, concat_axis=0, tiled=True)  111 us
    pallas_call x8, Pallas kernels, run_mix_in(): pl.pallas_call(functools.partial(mix_in_kernel, folds, near, cols, width,...  52.1 us
    pallas_call x5, Pallas kernels, run_mix_out(): pl.pallas_call(functools.partial(mix_out_kernel, folds, near, cols, width...  46.5 us
    all_to_all x8, starting transfers between devices, exchange(): return lax.all_to_all(array, EVERY, split_axis=0, concat_axis=0, tiled=True)  31.5 us
    all_to_all x8, waiting for transfers between devices, exchange(): return lax.all_to_all(array, EVERY, split_axis=0, concat_axis=0, tiled=True)  30.8 us
    pallas_call x3, Pallas kernels, run_projections(): pl.pallas_call(project_kernel, grid=(positions // step,), in_specs=[pl.Bl...  18.4 us
    pallas_call x2, Pallas kernels, run_finish(): pl.pallas_call(functools.partial(finish_kernel, len(mixes), onward is not...  15.5 us
  transfers between devices with their start and end apart: 16, of which 11 were waited for; matrix products, arithmetic and copies ran while one was open for 2% of the time, Pallas kernels for 23%

profile of v1, /device:TPU:0, one launch (start us, length us, event | category | flops | bytes accessed | tf_op | source)
XLA Modules:
  0.0 484.9 jit_solution(16844332465976547657)
XLA Ops:
  1.9 6.8 %project.3 = (bf16[8,8,9216]{2,1,0:T(8,128)(2,1)}, bf16[8,8,9216]{2,1,0:T(8,128)(2,1)}, bf16[8,8,9216]{2,1,0:T(8,128)(2,1)}, bf16[8,4,9216]{2,1,0:T(4,128)(2,1)}) custom-call(bf16[9216,128]{1,0:T(8,128)(2,1)} %bitcast.93, f32[1,128]{1,0:T(1,128)} %bitcast.116, bf16[448,128]{1,0:T(8,128)(2,1)} %copy-done.8), custom_call_target="tpu_custom_call" | custom-call | tf_op jit(solution)/shard_map/project/pallas_call | solution.py:163
  23.5 14.5 %all_to_all.70.refs_1_ = bf16[8,4,9216]{2,1,0:T(4,128)(2,1)} all-to-all(bf16[8,4,9216]{2,1,0:T(4,128)(2,1)} %project.4), channel_id=1, replica_groups=mesh['groups'=2,'far'=2,'near'=2,'chan'=2,'sub'=2] {'near','chan','sub'}, dimensions={0} | all-to-all | bytes 1179648 | tf_op jit(solution)/shard_map/all_to_all | solution.py:476
  38.0 19.1 %all_to_all.71.refs_0_.refs_1_ = bf16[8,8,9216]{2,1,0:T(8,128)(2,1)S(1)} all-to-all(bf16[8,8,9216]{2,1,0:T(8,128)(2,1)S(1)} %copy-done.5), channel_id=1, replica_groups=mesh['groups'=2,'far'=2,'near'=2,'chan'=2,'sub'=2] {'near','chan','sub'}, dimensions={0} | all-to-all | bytes 2359296 | tf_op jit(solution)/shard_map/all_to_all | solution.py:476
  57.1 18.9 %all_to_all.72.refs_1_.refs_0_ = bf16[8,8,9216]{2,1,0:T(8,128)(2,1)S(1)} all-to-all(bf16[8,8,9216]{2,1,0:T(8,128)(2,1)S(1)} %copy-done.4), channel_id=1, replica_groups=mesh['groups'=2,'far'=2,'near'=2,'chan'=2,'sub'=2] {'near','chan','sub'}, dimensions={0} | all-to-all | bytes 2359296 | tf_op jit(solution)/shard_map/all_to_all | solution.py:476
  86.5 7.1 %mix_out.7 = (bf16[8,4,9216]{2,1,0:T(4,128)(2,1)}, bf16[3072,128]{1,0:T(8,128)(2,1)}) custom-call(s32[2]{0:T(128)} %pad_add_fusion.half_ref, bf16[8,4,9216]{2,1,0:T(4,128)(2,1)S(1)} %copy-done.3, bf16[8,8,9216]{2,1,0:T(8,128)(2,1)S(1)} %all_to_all.72.refs_1_.refs_0_), custom_call_target="tpu_custom_call" | custom-call | tf_op jit(solution)/shard_map/mix_out/pallas_call | solution.py:412
  93.6 29.9 %collective-permute-done.3.refs_2_ = bf16[8,4,9216]{2,1,0:T(4,128)(2,1)} collective-permute-done((bf16[8,4,9216]{2,1,0:T(4,128)(2,1)}, bf16[8,4,9216]{2,1,0:T(4,128)(2,1)}, u32[]{:S(2)}, u32[]{:S(2)}) %collective-permute-start.3) | collective-permute-done | bytes 589856 | tf_op jit(solution)/shard_map/ppermute | solution.py:480
  123.5 10.7 %mix_out.8.refs_3_ = bf16[8,4,9216]{2,1,0:T(4,128)(2,1)} custom-call(s32[2]{0:T(128)} %pad_add_fusion.half_ref, bf16[8,8,9216]{2,1,0:T(8,128)(2,1)S(1)} %all_to_all.72.refs_1_.refs_0_, bf16[8,8,9216]{2,1,0:T(8,128)(2,1)S(1)} %all_to_all.71.refs_0_.refs_1_, bf16[8,4,9216]{2,1,0:T(4,128)(2,1)} %collective-permute-done.3.refs_2_), custom_call_target="tpu_custom_call" | custom-call | tf_op jit(solution)/shard_map/mix_out/pallas_call | solution.py:412
  135.6 6.7 %mix_out.9 = bf16[8,8,9216]{2,1,0:T(8,128)(2,1)} custom-call(s32[2]{0:T(128)} %pad_add_fusion.half_ref, bf16[3072,128]{1,0:T(8,128)(2,1)} %get-tuple-element.20.refs_0_, bf16[8,4,9216]{2,1,0:T(4,128)(2,1)} %get-tuple-element.21.refs_1_, bf16[8,4,9216]{2,1,0:T(4,128)(2,1)} %collective-permute-done.2.refs_2_, bf16[8,4,9216]{2,1,0:T(4,128)(2,1)} %mix_out.8.refs_3_), custom_call_target="tpu_custom_call" | custom-call | tf_op jit(solution)/shard_map/mix_out/pallas_call | solution.py:412
  150.3 22.3 %collective-permute-done.1.refs_2_ = bf16[8,4,9216]{2,1,0:T(4,128)(2,1)} collective-permute-done((bf16[8,4,9216]{2,1,0:T(4,128)(2,1)}, bf16[8,4,9216]{2,1,0:T(4,128)(2,1)}, u32[]{:S(2)}, u32[]{:S(2)}) %collective-permute-start.1) | collective-permute-done | bytes 589856 | tf_op jit(solution)/shard_map/ppermute | solution.py:480
  173.6 10.6 %mix_out.5.refs_3_ = bf16[8,4,9216]{2,1,0:T(4,128)(2,1)} custom-call(s32[2]{0:T(128)} %pad_add_fusion.half_ref, bf16[8,8,9216]{2,1,0:T(8,128)(2,1)S(1)} %all-to-all-done.1.refs_0_.refs_1_, bf16[8,4,9216]{2,1,0:T(4,128)(2,1)S(1)} %copy-done.1, bf16[8,4,9216]{2,1,0:T(4,128)(2,1)} %collective-permute-done.1.refs_2_), custom_call_target="tpu_custom_call" | custom-call | tf_op jit(solution)/shard_map/mix_out/pallas_call | solution.py:412
  184.2 16.8 %collective-permute-done.refs_2_ = bf16[8,4,9216]{2,1,0:T(4,128)(2,1)} collective-permute-done((bf16[8,4,9216]{2,1,0:T(4,128)(2,1)}, bf16[8,4,9216]{2,1,0:T(4,128)(2,1)}, u32[]{:S(2)}, u32[]{:S(2)}) %collective-permute-start) | collective-permute-done | bytes 589856 | tf_op jit(solution)/shard_map/ppermute | solution.py:480
  201.0 11.4 %mix_out.6 = bf16[8,8,9216]{2,1,0:T(8,128)(2,1)} custom-call(s32[2]{0:T(128)} %pad_add_fusion.half_ref, bf16[8,8,9216]{2,1,0:T(8,128)(2,1)S(1)} %all_to_all.71.refs_0_.refs_1_, bf16[8,8,9216]{2,1,0:T(8,128)(2,1)S(1)} %all-to-all-done.1.refs_0_.refs_1_, bf16[8,4,9216]{2,1,0:T(4,128)(2,1)} %collective-permute-done.refs_2_, bf16[8,4,9216]{2,1,0:T(4,128)(2,1)} %mix_out.5.refs_3_), custom_call_target="tpu_custom_call" | custom-call | tf_op jit(solution)/shard_map/mix_out/pallas_call | solution.py:412
  218.7 13.1 %all-to-all-done.3.refs_0_ = bf16[8,8,9216]{2,1,0:T(8,128)(2,1)S(1)} async-done(((bf16[8,8,9216]{2,1,0:T(8,128)(2,1)}), bf16[8,8,9216]{2,1,0:T(8,128)(2,1)S(1)}, u32[]{:S(2)}, u32[]{:S(2)}) %all-to-all-start.3) | async-done | bytes 1179680 | tf_op jit(solution)/shard_map/all_to_all | solution.py:476
  231.8 8.5 %finish.2 = (bf16[9216,128]{1,0:T(8,128)(2,1)}, bf16[8,8,9216]{2,1,0:T(8,128)(2,1)}) custom-call(bf16[8,8,9216]{2,1,0:T(8,128)(2,1)S(1)} %all-to-all-done.3.refs_0_, bf16[8,8,9216]{2,1,0:T(8,128)(2,1)S(1)} %all-to-all-done.6.refs_1_, bf16[9216,128]{1,0:T(8,128)(2,1)} %bitcast.95, f32[1,128]{1,0:T(1,128)} %bitcast.118, bf16[128,128]{1,0:T(8,128)(2,1)} %refs_4_.1, ...), custom_call_target="tpu_custom_call" | custom-call | tf_op jit(solution)/shard_map/finish/pallas_call | solution.py:185
  240.3 6.5 %project.5 = (bf16[8,8,9216]{2,1,0:T(8,128)(2,1)}, bf16[8,8,9216]{2,1,0:T(8,128)(2,1)}, bf16[8,8,9216]{2,1,0:T(8,128)(2,1)}) custom-call(bf16[9216,128]{1,0:T(8,128)(2,1)} %get-tuple-element.23.state_ref.refs_3_, f32[1,128]{1,0:T(1,128)} %bitcast.120, bf16[384,128]{1,0:T(8,128)(2,1)} %copy-done.9), custom_call_target="tpu_custom_call" | custom-call | tf_op jit(solution)/shard_map/project/pallas_call | solution.py:163
  246.8 20.9 %all_to_all.73.both_ref = bf16[8,8,9216]{2,1,0:T(8,128)(2,1)} all-to-all(bf16[8,8,9216]{2,1,0:T(8,128)(2,1)} %get-tuple-element.26), channel_id=1, replica_groups=mesh['groups'=2,'far'=2,'near'=2,'chan'=2,'sub'=2] {'near','chan','sub'}, dimensions={0} | all-to-all | bytes 2359296 | tf_op jit(solution)/shard_map/all_to_all | solution.py:476
  267.7 19.1 %all_to_all.74.both_ref = bf16[8,8,9216]{2,1,0:T(8,128)(2,1)S(1)} all-to-all(bf16[8,8,9216]{2,1,0:T(8,128)(2,1)S(1)} %copy-done.7), channel_id=1, replica_groups=mesh['groups'=2,'far'=2,'near'=2,'chan'=2,'sub'=2] {'near','chan','sub'}, dimensions={0} | all-to-all | bytes 2359296 | tf_op jit(solution)/shard_map/all_to_all | solution.py:476
  286.8 18.9 %all_to_all.75.both_ref = bf16[8,8,9216]{2,1,0:T(8,128)(2,1)S(1)} all-to-all(bf16[8,8,9216]{2,1,0:T(8,128)(2,1)S(1)} %copy-done.6), channel_id=1, replica_groups=mesh['groups'=2,'far'=2,'near'=2,'chan'=2,'sub'=2] {'near','chan','sub'}, dimensions={0} | all-to-all | bytes 2359296 | tf_op jit(solution)/shard_map/all_to_all | solution.py:476
  310.6 6.4 %mix_in.15 = bf16[8,4,9216]{2,1,0:T(4,128)(2,1)} custom-call(s32[2]{0:T(128)} %pad_add_fusion.half_ref, bf16[8,8,9216]{2,1,0:T(8,128)(2,1)S(1)} %copy-done), custom_call_target="tpu_custom_call" | custom-call | tf_op jit(solution)/shard_map/mix_in/pallas_call | solution.py:452
  320.0 6.6 %mix_in.14.refs_0_ = f32[8,4,9216]{2,1,0:T(4,128)} custom-call(s32[2]{0:T(128)} %pad_add_fusion.half_ref, bf16[8,8,9216]{2,1,0:T(8,128)(2,1)S(1)} %copy-done), custom_call_target="tpu_custom_call" | custom-call | tf_op jit(solution)/shard_map/mix_in/pallas_call | solution.py:452
  326.6 20.2 %collective-permute-done.7.refs_1_ = bf16[8,4,9216]{2,1,0:T(4,128)(2,1)S(1)} collective-permute-done((bf16[8,4,9216]{2,1,0:T(4,128)(2,1)}, bf16[8,4,9216]{2,1,0:T(4,128)(2,1)S(1)}, u32[]{:S(2)}, u32[]{:S(2)}) %collective-permute-start.7) | collective-permute-done | bytes 589856 | tf_op jit(solution)/shard_map/ppermute | solution.py:480
  353.1 6.4 %mix_in.13 = bf16[8,4,9216]{2,1,0:T(4,128)(2,1)} custom-call(s32[2]{0:T(128)} %pad_add_fusion.half_ref, bf16[8,8,9216]{2,1,0:T(8,128)(2,1)S(1)} %all_to_all.74.both_ref), custom_call_target="tpu_custom_call" | custom-call | tf_op jit(solution)/shard_map/mix_in/pallas_call | solution.py:452
  361.8 6.6 %mix_in.12.refs_0_ = f32[8,4,9216]{2,1,0:T(4,128)} custom-call(s32[2]{0:T(128)} %pad_add_fusion.half_ref, bf16[8,8,9216]{2,1,0:T(8,128)(2,1)S(1)} %all_to_all.74.both_ref), custom_call_target="tpu_custom_call" | custom-call | tf_op jit(solution)/shard_map/mix_in/pallas_call | solution.py:452
  368.4 20.5 %collective-permute-done.6.refs_1_ = bf16[8,4,9216]{2,1,0:T(4,128)(2,1)S(1)} collective-permute-done((bf16[8,4,9216]{2,1,0:T(4,128)(2,1)}, bf16[8,4,9216]{2,1,0:T(4,128)(2,1)S(1)}, u32[]{:S(2)}, u32[]{:S(2)}) %collective-permute-start.6) | collective-permute-done | bytes 589856 | tf_op jit(solution)/shard_map/ppermute | solution.py:480
  394.7 6.4 %mix_in.11 = bf16[8,4,9216]{2,1,0:T(4,128)(2,1)} custom-call(s32[2]{0:T(128)} %pad_add_fusion.half_ref, bf16[8,8,9216]{2,1,0:T(8,128)(2,1)S(1)} %all_to_all.75.both_ref), custom_call_target="tpu_custom_call" | custom-call | tf_op jit(solution)/shard_map/mix_in/pallas_call | solution.py:452
  403.6 6.4 %mix_in.9 = bf16[8,4,9216]{2,1,0:T(4,128)(2,1)} custom-call(s32[2]{0:T(128)} %pad_add_fusion.half_ref, bf16[8,8,9216]{2,1,0:T(8,128)(2,1)S(1)} %all-to-all-done.7.both_ref), custom_call_target="tpu_custom_call" | custom-call | tf_op jit(solution)/shard_map/mix_in/pallas_call | solution.py:452
  410.5 6.6 %mix_in.10.refs_2_ = f32[8,4,9216]{2,1,0:T(4,128)} custom-call(s32[2]{0:T(128)} %pad_add_fusion.half_ref, bf16[8,8,9216]{2,1,0:T(8,128)(2,1)S(1)} %all_to_all.75.both_ref), custom_call_target="tpu_custom_call" | custom-call | tf_op jit(solution)/shard_map/mix_in/pallas_call | solution.py:452
  417.1 6.6 %mix_in.8.refs_0_ = f32[8,4,9216]{2,1,0:T(4,128)} custom-call(s32[2]{0:T(128)} %pad_add_fusion.half_ref, bf16[8,8,9216]{2,1,0:T(8,128)(2,1)S(1)} %all-to-all-done.7.both_ref), custom_call_target="tpu_custom_call" | custom-call | tf_op jit(solution)/shard_map/mix_in/pallas_call | solution.py:452
  423.7 20.0 %collective-permute-done.5.refs_3_ = bf16[8,4,9216]{2,1,0:T(4,128)(2,1)S(1)} collective-permute-done((bf16[8,4,9216]{2,1,0:T(4,128)(2,1)}, bf16[8,4,9216]{2,1,0:T(4,128)(2,1)S(1)}, u32[]{:S(2)}, u32[]{:S(2)}) %collective-permute-start.5) | collective-permute-done | bytes 589856 | tf_op jit(solution)/shard_map/ppermute | solution.py:480
  443.7 12.0 %collective-permute-done.4.refs_1_ = bf16[8,4,9216]{2,1,0:T(4,128)(2,1)S(1)} collective-permute-done((bf16[8,4,9216]{2,1,0:T(4,128)(2,1)}, bf16[8,4,9216]{2,1,0:T(4,128)(2,1)S(1)}, u32[]{:S(2)}, u32[]{:S(2)}) %collective-permute-start.4) | collective-permute-done | bytes 589856 | tf_op jit(solution)/shard_map/ppermute | solution.py:480
  463.9 13.9 %all-to-all-done.9.refs_0_ = bf16[8,8,9216]{2,1,0:T(8,128)(2,1)S(1)} async-done(((bf16[8,8,9216]{2,1,0:T(8,128)(2,1)}), bf16[8,8,9216]{2,1,0:T(8,128)(2,1)S(1)}, u32[]{:S(2)}, u32[]{:S(2)}) %all-to-all-start.9) | async-done | bytes 1179680 | tf_op jit(solution)/shard_map/all_to_all | solution.py:476
  477.8 7.0 %finish.3 = bf16[9216,128]{1,0:T(8,128)(2,1)} custom-call(bf16[8,8,9216]{2,1,0:T(8,128)(2,1)S(1)} %all-to-all-done.9.refs_0_, bf16[8,4,9216]{2,1,0:T(4,128)(2,1)S(1)} %all-to-all-done.11.refs_1_, bf16[8,4,9216]{2,1,0:T(4,128)(2,1)} %all-to-all-done.13.refs_2_, bf16[9216,128]{1,0:T(8,128)(2,1)} %get-tuple-element.23.state_ref.refs_3_, f32[1,128]{1,0:T(1,128)} %bitcast.121, ...), custom_call_target="tpu_custom_call" | custom-call | tf_op jit(solution)/shard_map/finish/pallas_call | solution.py:185
  (105 shorter events, 77.2 us)
Async XLA Ops:
  1.3 0.6 copy-start.8
  8.7 14.8 %all-to-all-start.4 = ((bf16[8,4,9216]{2,1,0:T(4,128)(2,1)}), bf16[8,4,9216]{2,1,0:T(4,128)(2,1)S(1)}, u32[]{:S(2)}, u32[]{:S(2)}) async-start(bf16[8,4,9216]{2,1,0:T(4,128)(2,1)} %get-tuple-element.18), calls=%async_computation.4 | async-start | bytes 1179648 | tf_op jit(solution)/shard_map/all_to_all | solution.py:476
  19.7 18.3 %copy-start.5 = (bf16[8,8,9216]{2,1,0:T(8,128)(2,1)S(1)}, bf16[8,8,9216]{2,1,0:T(8,128)(2,1)}, u32[]{:S(2)}) copy-start(bf16[8,8,9216]{2,1,0:T(8,128)(2,1)} %get-tuple-element.16) | copy-start | bytes 3538948
  23.5 33.6 %copy-start.2 = (bf16[8,4,9216]{2,1,0:T(4,128)(2,1)}, bf16[8,4,9216]{2,1,0:T(4,128)(2,1)S(1)}, u32[]{:S(2)}) copy-start(bf16[8,4,9216]{2,1,0:T(4,128)(2,1)S(1)} %all-to-all-done.4.refs_0_) | copy-start | bytes 1769476
  38.0 19.1 %copy-start.4 = (bf16[8,8,9216]{2,1,0:T(8,128)(2,1)S(1)}, bf16[8,8,9216]{2,1,0:T(8,128)(2,1)}, u32[]{:S(2)}) copy-start(bf16[8,8,9216]{2,1,0:T(8,128)(2,1)} %get-tuple-element.19) | copy-start | bytes 3538948
  76.1 66.2 %all-to-all-start.1 = ((bf16[8,8,9216]{2,1,0:T(8,128)(2,1)}), bf16[8,8,9216]{2,1,0:T(8,128)(2,1)S(1)}, u32[]{:S(2)}, u32[]{:S(2)}) async-start(bf16[8,8,9216]{2,1,0:T(8,128)(2,1)} %get-tuple-element.17), calls=%async_computation.1 | async-start | bytes 2359296 | tf_op jit(solution)/shard_map/all_to_all | solution.py:476
  80.8 42.7 %collective-permute-start.3 = (bf16[8,4,9216]{2,1,0:T(4,128)(2,1)}, bf16[8,4,9216]{2,1,0:T(4,128)(2,1)}, u32[]{:S(2)}, u32[]{:S(2)}) collective-permute-start(bf16[8,4,9216]{2,1,0:T(4,128)(2,1)} %slice.192), channel_id=1, source_target_pairs={{0,8},{8,0},{1,9},{9,1},{2,10},{10,2},{3,11},{11,3},{4,12},{12,4},... | collective-permute-start | bytes 1769480 | tf_op jit(solution)/shard_map/ppermute | solution.py:480
  84.5 51.1 %collective-permute-start.2 = (bf16[8,4,9216]{2,1,0:T(4,128)(2,1)}, bf16[8,4,9216]{2,1,0:T(4,128)(2,1)}, u32[]{:S(2)}, u32[]{:S(2)}) collective-permute-start(bf16[8,4,9216]{2,1,0:T(4,128)(2,1)} %slice.191), channel_id=1, source_target_pairs={{0,8},{8,0},{1,9},{9,1},{2,10},{10,2},{3,11},{11,3},{4,12},{12,4},... | collective-permute-start | bytes 1769480 | tf_op jit(solution)/shard_map/ppermute | solution.py:480
  85.4 1.1 copy-start.3
  142.3 70.1 %all-to-all-start.6 = ((bf16[8,8,9216]{2,1,0:T(8,128)(2,1)}), bf16[8,8,9216]{2,1,0:T(8,128)(2,1)S(1)}, u32[]{:S(2)}, u32[]{:S(2)}) async-start(bf16[8,8,9216]{2,1,0:T(8,128)(2,1)} %mix_out.9), calls=%async_computation.6 | async-start | bytes 2359296 | tf_op jit(solution)/shard_map/all_to_all | solution.py:476
  145.8 4.1 copy-start.13
  145.8 26.7 %collective-permute-start.1 = (bf16[8,4,9216]{2,1,0:T(4,128)(2,1)}, bf16[8,4,9216]{2,1,0:T(4,128)(2,1)}, u32[]{:S(2)}, u32[]{:S(2)}) collective-permute-start(bf16[8,4,9216]{2,1,0:T(4,128)(2,1)} %all_to_all.70.refs_1_), channel_id=1, source_target_pairs={{0,8},{8,0},{1,9},{9,1},{2,10},{10,2},{3,11},{11,3},{4,12},{12,4},... | collective-permute-start | bytes 1769480 | tf_op jit(solution)/shard_map/ppermute | solution.py:480
  149.9 51.1 %collective-permute-start = (bf16[8,4,9216]{2,1,0:T(4,128)(2,1)}, bf16[8,4,9216]{2,1,0:T(4,128)(2,1)}, u32[]{:S(2)}, u32[]{:S(2)}) collective-permute-start(bf16[8,4,9216]{2,1,0:T(4,128)(2,1)} %slice.188), channel_id=1, source_target_pairs={{0,8},{8,0},{1,9},{9,1},{2,10},{10,2},{3,11},{11,3},{4,12},{12,4},... | collective-permute-start | bytes 1769480 | tf_op jit(solution)/shard_map/ppermute | solution.py:480
  172.5 1.1 copy-start.1
  212.3 4.0 copy-start.10
  212.3 19.5 %all-to-all-start.3 = ((bf16[8,8,9216]{2,1,0:T(8,128)(2,1)}), bf16[8,8,9216]{2,1,0:T(8,128)(2,1)S(1)}, u32[]{:S(2)}, u32[]{:S(2)}) async-start(bf16[8,8,9216]{2,1,0:T(8,128)(2,1)} %mix_out.6), calls=%async_computation.3 | async-start | bytes 2359296 | tf_op jit(solution)/shard_map/all_to_all | solution.py:476
  216.2 1.9 copy-start.11
  217.5 22.9 %copy-start.9 = (bf16[384,128]{1,0:T(8,128)(2,1)}, bf16[384,128]{1,0:T(8,128)(2,1)S(1)}, u32[]{:S(2)}) copy-start(bf16[384,128]{1,0:T(8,128)(2,1)S(1)} %constant_dynamic-update-slice_fusion.8.rows_ref) | copy-start | bytes 294916
  246.8 20.9 %copy-start.7 = (bf16[8,8,9216]{2,1,0:T(8,128)(2,1)S(1)}, bf16[8,8,9216]{2,1,0:T(8,128)(2,1)}, u32[]{:S(2)}) copy-start(bf16[8,8,9216]{2,1,0:T(8,128)(2,1)} %get-tuple-element.25) | copy-start | bytes 3538948
  267.7 19.1 %copy-start.6 = (bf16[8,8,9216]{2,1,0:T(8,128)(2,1)S(1)}, bf16[8,8,9216]{2,1,0:T(8,128)(2,1)}, u32[]{:S(2)}) copy-start(bf16[8,8,9216]{2,1,0:T(8,128)(2,1)} %get-tuple-element.24) | copy-start | bytes 3538948
  305.8 43.1 %all-to-all-start.7 = ((bf16[8,8,9216]{2,1,0:T(8,128)(2,1)}), bf16[8,8,9216]{2,1,0:T(8,128)(2,1)S(1)}, u32[]{:S(2)}, u32[]{:S(2)}) async-start(bf16[8,8,9216]{2,1,0:T(8,128)(2,1)} %get-tuple-element.22), calls=%async_computation.7 | async-start | bytes 2359296 | tf_op jit(solution)/shard_map/all_to_all | solution.py:476
  309.3 1.3 copy-start
  317.0 29.7 %collective-permute-start.7 = (bf16[8,4,9216]{2,1,0:T(4,128)(2,1)}, bf16[8,4,9216]{2,1,0:T(4,128)(2,1)S(1)}, u32[]{:S(2)}, u32[]{:S(2)}) collective-permute-start(bf16[8,4,9216]{2,1,0:T(4,128)(2,1)} %mix_in.15), channel_id=1, source_target_pairs={{0,8},{8,0},{1,9},{9,1},{2,10},{10,2},{3,11},{11,3},{4,12},{12,4},... | collective-permute-start | bytes 1769480 | tf_op jit(solution)/shard_map/ppermute | solution.py:480
  348.9 42.1 %all-to-all-start.13 = ((bf16[8,4,9216]{2,1,0:T(4,128)(2,1)}), bf16[8,4,9216]{2,1,0:T(4,128)(2,1)}, u32[]{:S(2)}, u32[]{:S(2)}) async-start(bf16[8,4,9216]{2,1,0:T(4,128)(2,1)} %add.7), calls=%async_computation.13 | async-start | bytes 1179648 | tf_op jit(solution)/shard_map/all_to_all | solution.py:476
  359.5 29.4 %collective-permute-start.6 = (bf16[8,4,9216]{2,1,0:T(4,128)(2,1)}, bf16[8,4,9216]{2,1,0:T(4,128)(2,1)S(1)}, u32[]{:S(2)}, u32[]{:S(2)}) collective-permute-start(bf16[8,4,9216]{2,1,0:T(4,128)(2,1)} %mix_in.13), channel_id=1, source_target_pairs={{0,8},{8,0},{1,9},{9,1},{2,10},{10,2},{3,11},{11,3},{4,12},{12,4},... | collective-permute-start | bytes 1769480 | tf_op jit(solution)/shard_map/ppermute | solution.py:480
  391.0 67.4 %all-to-all-start.11 = ((bf16[8,4,9216]{2,1,0:T(4,128)(2,1)}), bf16[8,4,9216]{2,1,0:T(4,128)(2,1)S(1)}, u32[]{:S(2)}, u32[]{:S(2)}) async-start(bf16[8,4,9216]{2,1,0:T(4,128)(2,1)} %add.6), calls=%async_computation.11 | async-start | bytes 1179648 | tf_op jit(solution)/shard_map/all_to_all | solution.py:476
  401.1 42.6 %collective-permute-start.5 = (bf16[8,4,9216]{2,1,0:T(4,128)(2,1)}, bf16[8,4,9216]{2,1,0:T(4,128)(2,1)S(1)}, u32[]{:S(2)}, u32[]{:S(2)}) collective-permute-start(bf16[8,4,9216]{2,1,0:T(4,128)(2,1)} %mix_in.11), channel_id=1, source_target_pairs={{0,8},{8,0},{1,9},{9,1},{2,10},{10,2},{3,11},{11,3},{4,12},{12,4},... | collective-permute-start | bytes 1769480 | tf_op jit(solution)/shard_map/ppermute | solution.py:480
  410.0 45.7 %collective-permute-start.4 = (bf16[8,4,9216]{2,1,0:T(4,128)(2,1)}, bf16[8,4,9216]{2,1,0:T(4,128)(2,1)S(1)}, u32[]{:S(2)}, u32[]{:S(2)}) collective-permute-start(bf16[8,4,9216]{2,1,0:T(4,128)(2,1)} %mix_in.9), channel_id=1, source_target_pairs={{0,8},{8,0},{1,9},{9,1},{2,10},{10,2},{3,11},{11,3},{4,12},{12,4},... | collective-permute-start | bytes 1769480 | tf_op jit(solution)/shard_map/ppermute | solution.py:480
  458.3 3.7 copy-start.14
  458.3 5.0 %copy-start.12 = (bf16[128,128]{1,0:T(8,128)(2,1)S(1)}, bf16[128,128]{1,0:T(8,128)(2,1)}, u32[]{:S(2)}) copy-start(bf16[128,128]{1,0:T(8,128)(2,1)} %param.21) | copy-start | bytes 98308
  458.3 19.5 %all-to-all-start.9 = ((bf16[8,8,9216]{2,1,0:T(8,128)(2,1)}), bf16[8,8,9216]{2,1,0:T(8,128)(2,1)S(1)}, u32[]{:S(2)}, u32[]{:S(2)}) async-start(bf16[8,8,9216]{2,1,0:T(8,128)(2,1)} %add.5), calls=%async_computation.9 | async-start | bytes 2359296 | tf_op jit(solution)/shard_map/all_to_all | solution.py:476
